TPU v7x, 256 devices: a whole 4x4x8 slice. The times are simulated.
256 devices in a mesh: row: 16 (over x_hi, z), col: 16 (over y, x_lo, core).
Axes of the slice: x: 4 (x_hi: 2, x_lo: 2; x = x_hi * 2 + x_lo), y: 4, z: 8, core: 2. Of those that a mesh axis runs over, the one named last changes fastest.
Arguments:
- panel_values: bfloat16 [65536, 256], P(('row', 'col')), may hold values from -6 to 6
- near_tiles: bfloat16 [8192, 256, 256], P(('row', 'col')), may hold values from -0.01953125 to 0.01953125
- far_left: bfloat16 [32768, 64, 256], P(('row', 'col')), may hold values from -0.0390625 to 0.0390625
- far_right: bfloat16 [32768, 64, 256], P(('row', 'col')), may hold values from -0.375 to 0.375
- near_rows: int32 [8192], P(('row', 'col')), may hold values from 0 to 255, as said below
- far_rows: int32 [32768], P(('row', 'col')), may hold values from 0 to 255, as said below
Outputs:
- panel_product: bfloat16 [65536, 256], P(('row', 'col'))
Inputs may be any that keep to these rules, and one draw needn't show every extreme that they name: `near_rows`: entries of the device at grid position (i, j) lie in its row group, clusters i * 16 * 1 to (i + 1) * 16 - 1. `far_rows`: entries of the device at grid position (i, j) lie in its row group, clusters i * 16 * 1 to (i + 1) * 16 - 1.
All inputs are finite; a program needn't handle non-finite values.
Results may differ from a plain program's by a relative error of at most 0.0046.
Values may be sent and summed in bfloat16 or wider, within the bound.
A program may use at most 192 MiB of HBM per device.

v0:
```python
import jax
import jax.numpy as jnp
from jax import lax
from jax.sharding import PartitionSpec as P

TILE = 256
RANK = 64
NRHS = 256
DPC = 2
LPC = 8


def back_part(near_tiles, far_left, far_right, near_input, far_input, count):
    near_out = jnp.einsum(
        "sij,sin->sjn", near_tiles, near_input, preferred_element_type=jnp.float32
    )
    near_sum = near_out.reshape(count, DPC, TILE, NRHS).sum(axis=1)
    coef = jnp.einsum(
        "skt,stn->skn", far_left, far_input, preferred_element_type=jnp.float32
    ).astype(jnp.bfloat16)
    far_out = jnp.einsum("skt,skn->stn", far_right, coef, preferred_element_type=jnp.float32)
    far_sum = far_out.reshape(count, LPC, TILE, NRHS).sum(axis=1)
    return (near_sum + far_sum).reshape(count * TILE, NRHS)


def forward_part(near_tiles, far_left, far_right, near_local, far_local, colx, count, groups):
    tiles = near_tiles.reshape(count, DPC, TILE, TILE)
    near_out = jnp.einsum("cdij,cjn->cdin", tiles, colx, preferred_element_type=jnp.float32)
    near_out = near_out.reshape(count * DPC, TILE, NRHS)
    right = far_right.reshape(count, LPC, RANK, TILE)
    coef = jnp.einsum("cdkt,ctn->cdkn", right, colx, preferred_element_type=jnp.float32).astype(
        jnp.bfloat16
    )
    left = far_left.reshape(count, LPC, RANK, TILE)
    far_out = jnp.einsum("cdkt,cdkn->cdtn", left, coef, preferred_element_type=jnp.float32)
    far_out = far_out.reshape(count * LPC, TILE, NRHS)
    total = jax.ops.segment_sum(near_out, near_local, num_segments=groups)
    total = total + jax.ops.segment_sum(far_out, far_local, num_segments=groups)
    return total.reshape(groups * TILE, NRHS)


def per_device(panel_values, near_tiles, far_left, far_right, near_rows, far_rows):
    n_row = lax.axis_size("row")
    n_col = lax.axis_size("col")
    clusters = panel_values.shape[0] // TILE
    groups = n_col * clusters
    colcount = n_row * clusters
    row_base = lax.axis_index("row") * groups
    near_local = near_rows - row_base
    far_local = far_rows - row_base
    row_slab = lax.all_gather(panel_values, "col", axis=0, tiled=True)
    rowx = row_slab.reshape(groups, TILE, NRHS)
    near_input = jnp.take(rowx, near_local, axis=0)
    far_input = jnp.take(rowx, far_local, axis=0)
    col_slab = lax.all_gather(panel_values, "row", axis=0, tiled=True)
    colx = col_slab.reshape(colcount, TILE, NRHS)
    forward = forward_part(
        near_tiles, far_left, far_right, near_local, far_local, colx, colcount, groups
    )
    backward = back_part(near_tiles, far_left, far_right, near_input, far_input, colcount)
    own_back = lax.psum_scatter(backward, "row", scatter_dimension=0, tiled=True)
    own_forward = lax.psum_scatter(forward, "col", scatter_dimension=0, tiled=True)
    return (own_forward + own_back).astype(jnp.bfloat16)


def solution(mesh):
    placed = (
        P(("row", "col"), None),
        P(("row", "col"), None, None),
        P(("row", "col"), None, None),
        P(("row", "col"), None, None),
        P(("row", "col")),
        P(("row", "col")),
    )
    return jax.shard_map(
        per_device, mesh=mesh, in_specs=placed, out_specs=P(("row", "col"), None), check_vma=False
    )
```

profile of v0, /device:TPU:32, one launch (start us, length us, event | category | flops | bytes accessed | tf_op | source)
XLA Modules:
  0.0 426.7 jit_solution(15875031635582271066)
XLA Ops:
  6.5 0.0 all-gather.5.cloned.1.call-start
  6.5 0.7 all-gather.5.cloned.1.call-update
  7.3 0.0 all-gather.3.cloned.1.call-start
  7.3 0.7 all-gather.3.cloned.1.call-update
  8.0 0.0 reduce-scatter.5.cloned.1.call-start
  8.1 0.7 compare_and_fusion
  8.7 0.7 compare_and_fusion.1
  9.4 38.9 %all-gather.5.cloned.1.call-done = bf16[4096,256]{1,0:T(8,128)(2,1)} async-done(((bf16[256,256]{1,0:T(8,128)(2,1)}), bf16[4096,256]{1,0:T(8,128)(2,1)}) %all-gather.5.cloned.1.call-update) | async-done | bytes 2097168 | tf_op jit(solution)/shard_map/all_gather | solution.py:51
  48.3 0.0 copy-start
  48.3 10.0 %gather_fusion.1 = bf16[128,256,256]{2,1,0:T(8,128)(2,1)} fusion(bf16[16,256,256]{2,1,0:T(8,128)(2,1)} %bitcast.32, s32[1024]{0:T(1024)S(1)} %pad_clamp_fusion), kind=kCustom, calls=%fused_computation.1 | custom fusion | bytes 33554944 | tf_op jit(solution)/shard_map/jit(_take)/gather | solution.py:54
  58.3 0.0 copy-done
  58.3 2.8 gather_fusion
  61.1 7.4 %bitcast_reduce_fusion.1 = f32[16,256,256]{1,2,0:T(8,128)} fusion(bf16[32,256,256]{2,1,0:T(8,128)(2,1)} %param.7, bf16[32,256,256]{2,1,0:T(8,128)(2,1)} %gather_fusion, pred[32]{0:T(512)(128)(4,1)S(1)} %get-tuple-element.7), kind=kOutput, calls=%fused_computation.8 | convolution fusion | flops 1076887552 | bytes 12582944 | tf_op jit(solution)/shard_map/sij,sin->sjn/dot_general | solution.py:14
  68.5 16.6 %bitcast_reduce_fusion = f32[16,256,256]{1,2,0:T(8,128)} fusion(bf16[128,64,256]{2,1,0:T(8,128)(2,1)} %param.9, bf16[128,64,256]{2,1,0:T(8,128)(2,1)} %param.8, bf16[128,256,256]{2,1,0:T(8,128)(2,1)} %gather_fusion.1, pred[128]{0:T(512)(128)(4,1)S(1)} %get-tuple-element.5), kind=kOutput, calls=%fused_computation.4 | convolution fusion | flops 2165309440 | bytes 29360256 | tf_op jit(solution)/shard_map/skt,skn->stn/dot_general | solution.py:21
  85.1 6.0 %add.42 = f32[16,256,256]{1,2,0:T(8,128)} add(f32[16,256,256]{1,2,0:T(8,128)} %bitcast_reduce_fusion.1, f32[16,256,256]{1,2,0:T(8,128)} %bitcast_reduce_fusion) | non-fusion elementwise | flops 1048576 | bytes 12582912 | tf_op jit(solution)/shard_map/add | solution.py:23
  91.1 5.3 %copy.13 = f32[16,256,256]{2,1,0:T(8,128)} copy(f32[16,256,256]{1,2,0:T(8,128)} %add.42) | data formatting | bytes 8388608 | tf_op jit(solution)/shard_map/add | solution.py:23
  96.4 0.0 reduce-scatter.5.cloned.1.call-update
  96.5 0.2 reduce-scatter.3.cloned.1.call-start
  96.7 39.2 %all-gather.3.cloned.1.call-done = bf16[4096,256]{1,0:T(8,128)(2,1)} async-done(((bf16[256,256]{1,0:T(8,128)(2,1)}), bf16[4096,256]{1,0:T(8,128)(2,1)}) %all-gather.3.cloned.1.call-update) | async-done | bytes 2097168 | tf_op jit(solution)/shard_map/all_gather | solution.py:55
  135.9 16.3 %fusion.16 = f32[16,8,256,256]{3,2,1,0:T(8,128)} fusion(bf16[16,8,64,256]{3,2,1,0:T(8,128)(2,1)} %bitcast.41, bf16[16,8,64,256]{3,2,1,0:T(8,128)(2,1)} %bitcast.40, bf16[16,256,256,1]{2,1,3,0:T(8,128)(2,1)} %bitcast.35), kind=kOutput, calls=%fused_computation.14 | convolution fusion | flops 2149580800 | bytes 44040192 | tf_op jit(solution)/shard_map/cdkt,cdkn->cdtn/dot_general | solution.py:35
  152.3 33.5 %copy.11 = f32[128,256,256]{2,1,0:T(8,128)} copy(f32[128,256,256]{1,2,0:T(8,128)} %bitcast.31) | data formatting | bytes 67108864 | tf_op jit(solution)/shard_map/reshape | solution.py:36
  185.8 2.5 broadcast.9.clone.1
  188.3 72.1 %scatter_fusion.1 = f32[16,256,256]{2,1,0:T(8,128)} fusion(f32[16,256,256]{2,1,0:T(8,128)} %broadcast.9.clone.1, s32[128]{0:T(128)S(1)} %get-tuple-element.6, f32[128,256,256]{2,1,0:T(8,128)} %copy.11), kind=kCustom, calls=%fused_computation.3 | custom fusion | flops 8388608 | bytes 100663808 | tf_op jit(solution)/shard_map/scatter-add | solution.py:38
  260.4 0.0 copy-done.1
  260.4 6.7 %fusion.27 = f32[16,2,256,256]{3,2,1,0:T(8,128)} fusion(bf16[16,2,256,256]{3,2,1,0:T(8,128)(2,1)} %bitcast.39, bf16[16,256,256,1]{2,1,3,0:T(8,128)(2,1)S(1)} %bitcast.36), kind=kOutput, calls=%fused_computation.30 | convolution fusion | flops 1073741824 | bytes 14680064 | tf_op jit(solution)/shard_map/cdij,cjn->cdin/dot_general | solution.py:28
  267.0 2.4 broadcast.9.clone
  269.4 18.2 %scatter_fusion = f32[16,256,256]{2,1,0:T(8,128)} fusion(f32[16,256,256]{2,1,0:T(8,128)} %broadcast.9.clone, s32[32]{0:T(128)S(1)} %get-tuple-element.8, f32[32,256,256]{2,1,0:T(8,128)} %bitcast.34), kind=kCustom, calls=%fused_computation.2 | custom fusion | flops 2097152 | bytes 25165952 | tf_op jit(solution)/shard_map/scatter-add | solution.py:37
  287.7 6.1 %add.37 = f32[16,256,256]{2,1,0:T(8,128)} add(f32[16,256,256]{2,1,0:T(8,128)} %scatter_fusion, f32[16,256,256]{2,1,0:T(8,128)} %scatter_fusion.1) | non-fusion elementwise | flops 1048576 | bytes 12582912 | tf_op jit(solution)/shard_map/add | solution.py:38
  293.7 0.0 reduce-scatter.3.cloned.1.call-update
  293.8 51.1 %reduce-scatter.5.cloned.1.call-done = f32[256,256]{1,0:T(8,128)} async-done(((f32[4096,256]{1,0:T(8,128)}), f32[256,256]{1,0:T(8,128)}) %reduce-scatter.5.cloned.1.call-update) | async-done | bytes 262160 | tf_op jit(solution)/shard_map/reduce_scatter | solution.py:61
  344.9 73.6 %reduce-scatter.3.cloned.1.call-done = f32[256,256]{1,0:T(8,128)} async-done(((f32[4096,256]{1,0:T(8,128)}), f32[256,256]{1,0:T(8,128)}) %reduce-scatter.3.cloned.1.call-update) | async-done | bytes 262160 | tf_op jit(solution)/shard_map/reduce_scatter | solution.py:62
  418.4 1.7 add_convert_fusion
  (5 shorter events, 0.0 us)
Async XLA Ops:
  6.5 41.8 %all-gather.5.cloned.1.call-start = ((), (), s32[]{:S(2)}) async-start(), calls=%async_computation.4 | async-start | bytes 2228224 | tf_op jit(solution)/shard_map/all_gather | solution.py:51
  7.3 128.7 %all-gather.3.cloned.1.call-start = ((), (), s32[]{:S(2)}) async-start(), calls=%async_computation.2 | async-start | bytes 2228224 | tf_op jit(solution)/shard_map/all_gather | solution.py:55
  8.0 336.9 %reduce-scatter.5.cloned.1.call-start = ((), (), s32[]{:S(2)}) async-start(), calls=%async_computation.5 | async-start | bytes 4456448 | tf_op jit(solution)/shard_map/reduce_scatter | solution.py:61
  48.3 10.0 %copy-start = (bf16[4096,256]{1,0:T(8,128)(2,1)S(1)}, bf16[4096,256]{1,0:T(8,128)(2,1)}, u32[]{:S(2)}) copy-start(bf16[4096,256]{1,0:T(8,128)(2,1)} %all-gather.5.cloned.1.call-done) | copy-start | bytes 6291460
  96.5 322.0 %reduce-scatter.3.cloned.1.call-start = ((), (), s32[]{:S(2)}) async-start(), calls=%async_computation.3 | async-start | bytes 4456448 | tf_op jit(solution)/shard_map/reduce_scatter | solution.py:62
  188.3 72.1 %copy-start.1 = (bf16[4096,256]{1,0:T(8,128)(2,1)S(1)}, bf16[4096,256]{1,0:T(8,128)(2,1)}, u32[]{:S(2)}) copy-start(bf16[4096,256]{1,0:T(8,128)(2,1)} %all-gather.3.cloned.1.call-done) | copy-start | bytes 6291460
Sparse Core Ops, SparseCore 0:
  9.2 39.0 all-gather.4
  50.9 84.9 all-gather.2
  140.0 204.8 reduce-scatter.4
  347.4 70.9 reduce-scatter.2
where the time goes:
time: 428 us; the launch traced here: 427 us
  waiting for transfers between devices  204 us (48%)
  other arithmetic  105 us (25%)
  local copies, waits for them, and re-layouts  56.6 us (13%)
  matrix products  47 us (11%)
  between operations  13.2 us (3%)
    reduce_scatter x1, waiting for transfers between devices, per_device(): lax.psum_scatter(forward, 'col', scatter_dimension=0, tiled=True)  73.6 us
    scatter-add x1, other arithmetic, forward_part(): total = total + jax.ops.segment_sum(far_out, far_local, num_segments=groups)  72.1 us
    reduce_scatter x1, waiting for transfers between devices, per_device(): lax.psum_scatter(backward, 'row', scatter_dimension=0, tiled=True)  51.1 us
    all_gather x1, waiting for transfers between devices, per_device(): col_slab = lax.all_gather(panel_values, 'row', axis=0, tiled=True)  39.2 us
    all_gather x1, waiting for transfers between devices, per_device(): row_slab = lax.all_gather(panel_values, 'col', axis=0, tiled=True)  38.9 us
    reshape x1, local copies, waits for them, and re-layouts, forward_part(): far_out = far_out.reshape(count * LPC, TILE, NRHS)  33.5 us
    scatter-add x1, other arithmetic, forward_part(): total = jax.ops.segment_sum(near_out, near_local, num_segments=groups)  18.2 us
    dot_general x1, matrix products, back_part(): jnp.einsum('skt,skn->stn', far_right, coef, preferred_element_type=jnp.fl...  16.6 us
  transfers between devices with their start and end apart: 4, of which 4 were waited for; matrix products, arithmetic and copies ran while one was open for 49% of the time, Pallas kernels for 0%

commit v1 on v0

--- a/solution.py
+++ b/solution.py
@@ -52,7 +52,9 @@
     rowx = row_slab.reshape(groups, TILE, NRHS)
     near_input = jnp.take(rowx, near_local, axis=0)
     far_input = jnp.take(rowx, far_local, axis=0)
-    col_slab = lax.all_gather(panel_values, "row", axis=0, tiled=True)
+    col_slab = jnp.concatenate(
+        lax.all_to_all(jnp.stack([panel_values] * lax.axis_size("row")), "row", 0, 0), axis=0
+    )
     colx = col_slab.reshape(colcount, TILE, NRHS)
     forward = forward_part(
         near_tiles, far_left, far_right, near_local, far_local, colx, colcount, groups

time: 428 us -> 411 us (0.960)
  waiting for transfers between devices: 204 us -> 108 us
  blocking collectives: 0 us -> 75.1 us
    all_to_all x0 -> x1, blocking collectives: none -> 75.1 us  [per_device(): lax.all_to_all(jnp.stack([panel_values] * lax.axis_size('row')), 'row', 0...]
    reduce_scatter x1, waiting for transfers between devices: 51.1 us -> 0.02 us  [per_device(): lax.psum_scatter(backward, 'row', scatter_dimension=0, tiled=True)]
    all_gather x1 -> x0, waiting for transfers between devices: 39.2 us -> none  [per_device(): col_slab = lax.all_gather(panel_values, 'row', axis=0, tiled=True)]
    reduce_scatter x1, waiting for transfers between devices: 73.6 us -> 67.5 us  [per_device(): lax.psum_scatter(forward, 'col', scatter_dimension=0, tiled=True)]
  transfers between devices with their start and end apart: 4 -> 3, of which waited for: 4 -> 2; matrix products, arithmetic and copies ran while one was open for 49% -> 40% of each run, Pallas kernels for 0% -> 0%
where the time goes in v1:
time: 411 us; the launch traced here: 410 us
  waiting for transfers between devices  108 us (26%)
  other arithmetic  105 us (26%)
  blocking collectives  75.1 us (18%)
  local copies, waits for them, and re-layouts  57.5 us (14%)
  matrix products  50.9 us (12%)
  between operations  13.1 us (3%)
    all_to_all x1, blocking collectives, per_device(): lax.all_to_all(jnp.stack([panel_values] * lax.axis_size('row')), 'row', 0...  75.1 us
    scatter-add x1, other arithmetic, forward_part(): total = total + jax.ops.segment_sum(far_out, far_local, num_segments=groups)  71.8 us
    reduce_scatter x1, waiting for transfers between devices, per_device(): lax.psum_scatter(forward, 'col', scatter_dimension=0, tiled=True)  67.5 us
    all_gather x1, waiting for transfers between devices, per_device(): row_slab = lax.all_gather(panel_values, 'col', axis=0, tiled=True)  39.6 us
    reshape x1, local copies, waits for them, and re-layouts, forward_part(): far_out = far_out.reshape(count * LPC, TILE, NRHS)  33.5 us
    dot_general x1, matrix products, forward_part(): jnp.einsum('cdkt,cdkn->cdtn', left, coef, preferred_element_type=jnp.floa...  20.4 us
    scatter-add x1, other arithmetic, forward_part(): total = jax.ops.segment_sum(near_out, near_local, num_segments=groups)  18.3 us
    dot_general x1, matrix products, back_part(): jnp.einsum('skt,skn->stn', far_right, coef, preferred_element_type=jnp.fl...  16.5 us
  transfers between devices with their start and end apart: 3, of which 2 were waited for; matrix products, arithmetic and copies ran while one was open for 40% of the time, Pallas kernels for 0%

profile of v1, /device:TPU:32, one launch (start us, length us, event | category | flops | bytes accessed | tf_op | source)
XLA Modules:
  0.0 409.8 jit_solution(4730845123740757307)
XLA Ops:
  6.5 0.0 all-gather.2.cloned.1.call-start
  6.5 0.7 all-gather.2.cloned.1.call-update
  7.3 0.0 reduce-scatter.5.cloned.1.call-start
  7.3 0.7 compare_and_fusion
  8.0 0.7 compare_and_fusion.1
  8.7 39.6 %all-gather.2.cloned.1.call-done = bf16[4096,256]{1,0:T(8,128)(2,1)} async-done(((bf16[256,256]{1,0:T(8,128)(2,1)}), bf16[4096,256]{1,0:T(8,128)(2,1)}) %all-gather.2.cloned.1.call-update) | async-done | bytes 2097168 | tf_op jit(solution)/shard_map/all_gather | solution.py:51
  48.3 0.0 copy-start
  48.3 10.0 %gather_fusion.1 = bf16[128,256,256]{2,1,0:T(8,128)(2,1)} fusion(bf16[16,256,256]{2,1,0:T(8,128)(2,1)} %bitcast.33, s32[1024]{0:T(1024)S(1)} %pad_clamp_fusion), kind=kCustom, calls=%fused_computation.1 | custom fusion | bytes 33554944 | tf_op jit(solution)/shard_map/jit(_take)/gather | solution.py:54
  58.3 0.0 copy-done
  58.3 2.8 gather_fusion
  61.1 7.3 %bitcast_reduce_fusion.1 = f32[16,256,256]{1,2,0:T(8,128)} fusion(bf16[32,256,256]{2,1,0:T(8,128)(2,1)} %param.7, bf16[32,256,256]{2,1,0:T(8,128)(2,1)} %gather_fusion, pred[32]{0:T(512)(128)(4,1)S(1)} %get-tuple-element.7), kind=kOutput, calls=%fused_computation.8 | convolution fusion | flops 1076887552 | bytes 12582944 | tf_op jit(solution)/shard_map/sij,sin->sjn/dot_general | solution.py:14
  68.4 16.5 %bitcast_reduce_fusion = f32[16,256,256]{1,2,0:T(8,128)} fusion(bf16[128,64,256]{2,1,0:T(8,128)(2,1)} %param.9, bf16[128,64,256]{2,1,0:T(8,128)(2,1)} %param.8, bf16[128,256,256]{2,1,0:T(8,128)(2,1)} %gather_fusion.1, pred[128]{0:T(512)(128)(4,1)S(1)} %get-tuple-element.5), kind=kOutput, calls=%fused_computation.4 | convolution fusion | flops 2165309440 | bytes 29360256 | tf_op jit(solution)/shard_map/skt,skn->stn/dot_general | solution.py:21
  84.9 6.0 %add.42 = f32[16,256,256]{1,2,0:T(8,128)} add(f32[16,256,256]{1,2,0:T(8,128)} %bitcast_reduce_fusion.1, f32[16,256,256]{1,2,0:T(8,128)} %bitcast_reduce_fusion) | non-fusion elementwise | flops 1048576 | bytes 12582912 | tf_op jit(solution)/shard_map/add | solution.py:23
  90.9 5.3 %copy.13 = f32[16,256,256]{2,1,0:T(8,128)} copy(f32[16,256,256]{1,2,0:T(8,128)} %add.42) | data formatting | bytes 8388608 | tf_op jit(solution)/shard_map/add | solution.py:23
  96.2 0.0 copy-start.1
  96.2 0.0 reduce-scatter.5.cloned.1.call-update
  96.3 0.0 reduce-scatter.3.cloned.1.call-start
  96.3 0.8 copy-done.1
  97.2 0.2 stack.2
  97.4 75.1 %all_to_all.5 = bf16[16,256,256]{2,1,0:T(8,128)(2,1)S(1)} all-to-all(bf16[16,256,256]{2,1,0:T(8,128)(2,1)S(1)} %stack.2), channel_id=1, replica_groups=mesh['row'=16,'col'=16] {'row'}, dimensions={0} | all-to-all | bytes 4194304 | tf_op jit(solution)/shard_map/all_to_all | solution.py:56
  172.4 20.4 %fusion.16 = f32[16,8,256,256]{3,2,1,0:T(8,128)} fusion(bf16[16,8,64,256]{3,2,1,0:T(8,128)(2,1)} %bitcast.40, bf16[16,8,64,256]{3,2,1,0:T(8,128)(2,1)} %bitcast.39, bf16[16,256,256]{2,1,0:T(8,128)(2,1)S(1)} %all_to_all.5), kind=kOutput, calls=%fused_computation.14 | convolution fusion | flops 2149580800 | bytes 44040192 | tf_op jit(solution)/shard_map/cdkt,cdkn->cdtn/dot_general | solution.py:35
  192.8 33.5 %copy.11 = f32[128,256,256]{2,1,0:T(8,128)} copy(f32[128,256,256]{1,2,0:T(8,128)} %bitcast.32) | data formatting | bytes 67108864 | tf_op jit(solution)/shard_map/reshape | solution.py:36
  226.3 2.5 broadcast.11.clone.1
  228.8 71.8 %scatter_fusion.1 = f32[16,256,256]{2,1,0:T(8,128)} fusion(f32[16,256,256]{2,1,0:T(8,128)} %broadcast.11.clone.1, s32[128]{0:T(128)S(1)} %get-tuple-element.6, f32[128,256,256]{2,1,0:T(8,128)} %copy.11), kind=kCustom, calls=%fused_computation.3 | custom fusion | flops 8388608 | bytes 100663808 | tf_op jit(solution)/shard_map/scatter-add | solution.py:38
  300.6 6.7 %fusion.23 = f32[16,2,256,256]{3,2,1,0:T(8,128)} fusion(bf16[16,2,256,256]{3,2,1,0:T(8,128)(2,1)} %bitcast.38, bf16[16,256,256]{2,1,0:T(8,128)(2,1)S(1)} %all_to_all.5), kind=kOutput, calls=%fused_computation.19 | convolution fusion | flops 1073741824 | bytes 14680064 | tf_op jit(solution)/shard_map/cdij,cjn->cdin/dot_general | solution.py:28
  307.3 2.4 broadcast.11.clone
  309.7 18.3 %scatter_fusion = f32[16,256,256]{2,1,0:T(8,128)} fusion(f32[16,256,256]{2,1,0:T(8,128)} %broadcast.11.clone, s32[32]{0:T(128)S(1)} %get-tuple-element.8, f32[32,256,256]{2,1,0:T(8,128)} %bitcast.35), kind=kCustom, calls=%fused_computation.2 | custom fusion | flops 2097152 | bytes 25165952 | tf_op jit(solution)/shard_map/scatter-add | solution.py:37
  328.0 6.0 %add.37 = f32[16,256,256]{2,1,0:T(8,128)} add(f32[16,256,256]{2,1,0:T(8,128)} %scatter_fusion, f32[16,256,256]{2,1,0:T(8,128)} %scatter_fusion.1) | non-fusion elementwise | flops 1048576 | bytes 12582912 | tf_op jit(solution)/shard_map/add | solution.py:38
  334.0 0.0 reduce-scatter.3.cloned.1.call-update
  334.1 0.0 reduce-scatter.5.cloned.1.call-done
  334.1 67.5 %reduce-scatter.3.cloned.1.call-done = f32[256,256]{1,0:T(8,128)} async-done(((f32[4096,256]{1,0:T(8,128)}), f32[256,256]{1,0:T(8,128)}) %reduce-scatter.3.cloned.1.call-update) | async-done | bytes 262160 | tf_op jit(solution)/shard_map/reduce_scatter | solution.py:64
  401.5 1.7 add_convert_fusion
  (4 shorter events, 0.0 us)
Async XLA Ops:
  6.5 41.8 %all-gather.2.cloned.1.call-start = ((), (), s32[]{:S(2)}) async-start(), calls=%async_computation.4 | async-start | bytes 2228224 | tf_op jit(solution)/shard_map/all_gather | solution.py:51
  7.3 326.8 %reduce-scatter.5.cloned.1.call-start = ((), (), s32[]{:S(2)}) async-start(), calls=%async_computation.5 | async-start | bytes 4456448 | tf_op jit(solution)/shard_map/reduce_scatter | solution.py:63
  48.3 10.0 %copy-start = (bf16[4096,256]{1,0:T(8,128)(2,1)S(1)}, bf16[4096,256]{1,0:T(8,128)(2,1)}, u32[]{:S(2)}) copy-start(bf16[4096,256]{1,0:T(8,128)(2,1)} %all-gather.2.cloned.1.call-done) | copy-start | bytes 6291460
  96.2 0.9 copy-start.1
  96.3 305.3 %reduce-scatter.3.cloned.1.call-start = ((), (), s32[]{:S(2)}) async-start(), calls=%async_computation.3 | async-start | bytes 4456448 | tf_op jit(solution)/shard_map/reduce_scatter | solution.py:64
Sparse Core Ops, SparseCore 0:
  9.2 39.0 all-gather.1
  96.4 228.4 reduce-scatter.4
  334.2 67.3 reduce-scatter.2
